TPU v7x, 512 devices: a whole 4x4x16 slice. The times are simulated.
512 devices in a mesh: dp: 32 (over z_lo, y), mp: 16 (over z_hi, x, core).
Axes of the slice: x: 4, y: 4, z: 16 (z_hi: 2, z_lo: 8; z = z_hi * 8 + z_lo), core: 2. Of those that a mesh axis runs over, the one named last changes fastest.
Arguments:
- hidden_in: bfloat16 [12288, 2048], P(('dp', 'mp')), may hold values from -12 to 12
- segment_ids: int32 [32, 384], P('dp'), may hold values from 0 to 7, never falling along the last dimension, each value on 1 to 192 neighbouring positions
- page_table: int32 [32, 3], P('dp'), may hold values from 0 to 2, each once within a row
- qkv_master: float32 [2048, 6144], P(('dp', 'mp')), may hold values from -0.3 to 0.3
- up_master: float32 [2048, 8192], P(('dp', 'mp')), may hold values from -0.125 to 0.125
- dense_weight: bfloat16 [2048, 2048], P('mp'), may hold values from -0.125 to 0.125
Outputs:
- hidden_out: bfloat16 [12288, 2048], P(('dp', 'mp'))
- activated: bfloat16 [12288, 8192], P('dp', 'mp')
- cache_pages: bfloat16 [96, 2, 16, 128, 128], P('dp', None, 'mp')
Inputs may be any that keep to these rules, and one draw needn't show every extreme that they name: `segment_ids`: within a group segment ids never fall; each request holds 1 to 192 tokens and one holds exactly that many. `page_table`: each row names every slot of its group once.
All inputs are finite; a program needn't handle non-finite values.
Results may differ from a plain program's by a relative error of at most 0.015.
Values may be sent and summed in bfloat16 or wider, within the bound.
A program may use at most 64 MiB of HBM per device.

v0:
```python
import jax
import jax.numpy as jnp
from jax import lax
from jax.sharding import PartitionSpec as P

H = 16
HD = 128
PAGE = 128


def layer_norm(values):
    mean_val = jnp.mean(values, -1, keepdims=True)
    centered = values - mean_val
    variance = jnp.mean(centered * centered, -1, keepdims=True)
    return centered * lax.rsqrt(variance + 1e-05)


def reorder_rows(weights, mp_count, dp_count):
    block = weights.shape[0] // (mp_count * dp_count)
    shaped = weights.reshape(mp_count, dp_count, block, weights.shape[1])
    return shaped.transpose(1, 0, 2, 3).reshape(weights.shape[0], weights.shape[1])


def attend(normed, qkv_w, segment, table, mp_index):
    group_rows = normed.shape[0]
    heads_dev = qkv_w.shape[1] // (3 * HD)
    joined = jnp.dot(normed, qkv_w, preferred_element_type=jnp.float32).astype(jnp.bfloat16)
    joined = joined.reshape(group_rows, heads_dev, 3, HD)
    query = joined[:, :, 0]
    keys = joined[:, :, 1]
    vals = joined[:, :, 2]
    head_ids = mp_index * heads_dev + jnp.arange(heads_dev)
    slopes = jnp.exp2(-8.0 * (head_ids + 1).astype(jnp.float32) / H)
    positions = jnp.arange(group_rows)
    distance = (positions[:, None] - positions[None, :]).astype(jnp.float32)
    allowed = (segment[:, None] == segment[None, :]) & (distance >= 0)
    scores = jnp.einsum("thd,shd->hts", query, keys, preferred_element_type=jnp.float32) / jnp.sqrt(
        jnp.float32(HD)
    )
    scores = scores - slopes[:, None, None] * distance[None]
    scores = jnp.where(allowed[None], scores, -jnp.inf)
    probs = jax.nn.softmax(scores, axis=-1).astype(jnp.bfloat16)
    context = jnp.einsum("hts,shd->thd", probs, vals, preferred_element_type=jnp.float32).astype(
        jnp.bfloat16
    )
    context = context.reshape(group_rows, heads_dev * HD)
    key_vals = jnp.stack([keys, vals], 1)
    pages_here = group_rows // PAGE
    key_vals = key_vals.reshape(pages_here, PAGE, 2, heads_dev, HD).transpose(0, 2, 3, 1, 4)
    cache = jnp.zeros((pages_here, 2, heads_dev, PAGE, HD), jnp.bfloat16).at[table].set(key_vals)
    return (context, cache)


def local(hidden_in, segment_ids, page_table, qkv_master, up_master, dense_weight):
    mp_count = lax.axis_size("mp")
    dp_count = lax.axis_size("dp")
    mp_index = lax.axis_index("mp")
    qkv_bf = qkv_master.astype(jnp.bfloat16)
    up_bf = up_master.astype(jnp.bfloat16)
    qkv_rows, up_rows = (
        lax.all_gather(qkv_bf, "dp", axis=0, tiled=True),
        lax.all_gather(up_bf, "dp", axis=0, tiled=True),
    )
    qkv_cols, up_cols = (
        lax.all_to_all(qkv_rows, "mp", split_axis=1, concat_axis=0, tiled=True),
        lax.all_to_all(up_rows, "mp", split_axis=1, concat_axis=0, tiled=True),
    )
    qkv_w = reorder_rows(qkv_cols, mp_count, dp_count)
    up_w = reorder_rows(up_cols, mp_count, dp_count)
    normed_own = layer_norm(hidden_in.astype(jnp.float32)).astype(jnp.bfloat16)
    normed = lax.all_gather(normed_own, "mp", axis=0, tiled=True)
    context, cache = attend(normed, qkv_w, segment_ids[0], page_table[0], mp_index)
    share = lax.psum_scatter(
        jnp.dot(context, dense_weight, preferred_element_type=jnp.float32).astype(jnp.bfloat16),
        "mp",
        scatter_dimension=0,
        tiled=True,
    ).astype(jnp.float32)
    stream_own = hidden_in.astype(jnp.float32) + share
    normed_two = lax.all_gather(
        layer_norm(stream_own).astype(jnp.bfloat16), "mp", axis=0, tiled=True
    )
    upper = jnp.dot(normed_two, up_w, preferred_element_type=jnp.float32)
    activated = jax.nn.gelu(upper, approximate=True).astype(jnp.bfloat16)
    return (stream_own.astype(jnp.bfloat16), activated, cache)


def solution(mesh):
    placed = (
        P(("dp", "mp"), None),
        P("dp", None),
        P("dp", None),
        P(("dp", "mp"), None),
        P(("dp", "mp"), None),
        P("mp", None),
    )
    return jax.shard_map(
        local,
        mesh=mesh,
        in_specs=placed,
        out_specs=(P(("dp", "mp"), None), P("dp", "mp"), P("dp", None, "mp", None, None)),
        check_vma=False,
    )
```

profile of v0, /device:TPU:1, one launch (start us, length us, event | category | flops | bytes accessed | tf_op | source)
XLA Modules:
  0.0 827.7 jit_solution(535030976519693917)
XLA Ops:
  7.2 0.0 copy-start
  7.2 0.0 all-gather.11.cloned.1.call-start
  7.2 1.6 convert_bitcast_fusion.1
  8.8 0.0 all-gather.11.cloned.1.call-update
  8.8 0.0 all-gather.13.cloned.1.call-start
  8.9 1.6 convert_bitcast_fusion
  10.4 0.0 all-gather.13.cloned.1.call-update
  10.5 207.6 %all-gather.11.cloned.1.call-done = bf16[32,4,6144]{2,1,0:T(4,128)(2,1)} async-done(((bf16[1,4,6144]{2,1,0:T(4,128)(2,1)}), bf16[32,4,6144]{2,1,0:T(4,128)(2,1)}) %all-gather.11.cloned.1.call-update) | async-done | bytes 1572880 | tf_op jit(solution)/shard_map/all_gather | solution.py:61
  218.1 3.1 all_to_all.24
  221.1 1.6 copy.20
  222.7 54.5 %all-to-all-start = ((bf16[128,16,384]{2,0,1:T(8,128)(2,1)}), bf16[128,16,384]{2,0,1:T(8,128)(2,1)}, u32[]{:S(2)}, u32[]{:S(2)}) async-start(bf16[128,16,384]{2,0,1:T(8,128)(2,1)} %copy.20), calls=%async_computation | async-start | bytes 3145728 | tf_op jit(solution)/shard_map/all_to_all | solution.py:65
  277.2 0.0 all-gather.7.cloned.1.call-start
  277.3 0.1 convert_reduce_fusion
  277.4 0.2 fusion.19
  277.7 0.7 fusion.20
  278.4 0.0 all-gather.7.cloned.1.call-update
  278.4 184.5 %all-gather.13.cloned.1.call-done = bf16[32,4,8192]{2,1,0:T(4,128)(2,1)} async-done(((bf16[1,4,8192]{2,1,0:T(4,128)(2,1)}), bf16[32,4,8192]{2,1,0:T(4,128)(2,1)}) %all-gather.13.cloned.1.call-update) | async-done | bytes 2097168 | tf_op jit(solution)/shard_map/all_gather | solution.py:62
  463.0 3.3 all_to_all.27
  466.2 2.5 copy.25
  468.7 0.0 all-to-all-done
  468.7 54.6 %all-to-all-start.1 = ((bf16[128,16,512]{2,0,1:T(8,128)(2,1)}), bf16[128,16,512]{2,0,1:T(8,128)(2,1)S(1)}, u32[]{:S(2)}, u32[]{:S(2)}) async-start(bf16[128,16,512]{2,0,1:T(8,128)(2,1)} %copy.25), calls=%async_computation.2 | async-start | bytes 4194304 | tf_op jit(solution)/shard_map/all_to_all | solution.py:66
  523.4 0.0 reduce-scatter.2.cloned.1.call-start
  523.5 2.3 copy.21
  525.8 2.0 copy.22
  527.8 3.7 reshape.134
  531.6 93.0 %all-gather.7.cloned.1.call-done = bf16[384,2048]{1,0:T(8,128)(2,1)} async-done(((bf16[24,2048]{1,0:T(8,128)(2,1)}), bf16[384,2048]{1,0:T(8,128)(2,1)}) %all-gather.7.cloned.1.call-update) | async-done | bytes 1572880 | tf_op jit(solution)/shard_map/all_gather | solution.py:71
  624.6 2.9 convolution_convert_fusion.1
  627.5 0.0 copy-start.3
  627.5 0.7 copy-done.3
  628.2 0.4 fusion.31
  628.6 0.1 fusion.12
  628.8 2.8 convolution_convert_fusion
  631.6 0.0 reduce-scatter.2.cloned.1.call-update
  631.6 0.2 all-gather.9.cloned.1.call-start
  631.9 103.5 %reduce-scatter.2.cloned.1.call-done = bf16[24,2048]{1,0:T(8,128)(2,1)} async-done(((bf16[384,2048]{1,0:T(8,128)(2,1)}), bf16[24,2048]{1,0:T(8,128)(2,1)}) %reduce-scatter.2.cloned.1.call-update) | async-done | bytes 98320 | tf_op jit(solution)/shard_map/reduce_scatter | solution.py:73
  735.4 1.0 fusion.21
  736.4 1.1 multiply_reduce_fusion
  737.5 1.6 multiply_convert_fusion
  739.1 0.0 all-gather.9.cloned.1.call-update
  739.2 0.1 copy.31
  739.3 0.1 copy.30
  739.6 0.8 scatter_fusion
  740.4 0.0 copy-start.2
  740.4 1.2 copy.26
  741.6 2.0 copy.27
  743.6 2.1 reshape.141
  745.6 71.5 %all-gather.9.cloned.1.call-done = bf16[384,2048]{1,0:T(8,128)(2,1)} async-done(((bf16[24,2048]{1,0:T(8,128)(2,1)}), bf16[384,2048]{1,0:T(8,128)(2,1)}) %all-gather.9.cloned.1.call-update) | async-done | bytes 1572880 | tf_op jit(solution)/shard_map/all_gather | solution.py:80
  817.2 3.9 fusion.10
  (21 shorter events, 0.2 us)
Async XLA Ops:
  7.2 621.6 %copy-start = (bf16[128,2048]{1,0:T(8,128)(2,1)S(1)}, bf16[128,2048]{1,0:T(8,128)(2,1)}, u32[]{:S(2)}) copy-start(bf16[128,2048]{1,0:T(8,128)(2,1)} %param.11) | copy-start | bytes 1572868
  7.2 210.9 %all-gather.11.cloned.1.call-start = ((), (), s32[]{:S(2)}) async-start(), calls=%async_computation.6 | async-start | bytes 1622016 | tf_op jit(solution)/shard_map/all_gather | solution.py:61
  8.8 454.1 %all-gather.13.cloned.1.call-start = ((), (), s32[]{:S(2)}) async-start(), calls=%async_computation.7 | async-start | bytes 2162688 | tf_op jit(solution)/shard_map/all_gather | solution.py:62
  222.7 54.6 %copy-start.1 = (bf16[24,2048]{1,0:T(8,128)(2,1)S(1)}, bf16[24,2048]{1,0:T(8,128)(2,1)}, u32[]{:S(2)}) copy-start(bf16[24,2048]{1,0:T(8,128)(2,1)} %param.6) | copy-start | bytes 294916
  222.7 246.0 %all-to-all-start = ((bf16[128,16,384]{2,0,1:T(8,128)(2,1)}), bf16[128,16,384]{2,0,1:T(8,128)(2,1)}, u32[]{:S(2)}, u32[]{:S(2)}) async-start(bf16[128,16,384]{2,0,1:T(8,128)(2,1)} %copy.20), calls=%async_computation | async-start | bytes 3145728 | tf_op jit(solution)/shard_map/all_to_all | solution.py:65
  277.2 347.4 %all-gather.7.cloned.1.call-start = ((), (), s32[]{:S(2)}) async-start(), calls=%async_computation.3 | async-start | bytes 1671168 | tf_op jit(solution)/shard_map/all_gather | solution.py:71
  468.7 54.7 %copy-start.5 = (s32[1,384]{1,0:T(1,128)S(1)}, s32[1,384]{1,0:T(1,128)}, u32[]{:S(2)}) copy-start(s32[1,384]{1,0:T(1,128)} %param.7) | copy-start | bytes 4612
  468.7 271.7 %all-to-all-start.1 = ((bf16[128,16,512]{2,0,1:T(8,128)(2,1)}), bf16[128,16,512]{2,0,1:T(8,128)(2,1)S(1)}, u32[]{:S(2)}, u32[]{:S(2)}) async-start(bf16[128,16,512]{2,0,1:T(8,128)(2,1)} %copy.25), calls=%async_computation.2 | async-start | bytes 4194304 | tf_op jit(solution)/shard_map/all_to_all | solution.py:66
  523.4 212.0 %reduce-scatter.2.cloned.1.call-start = ((), (), s32[]{:S(2)}) async-start(), calls=%async_computation.4 | async-start | bytes 1671168 | tf_op jit(solution)/shard_map/reduce_scatter | solution.py:73
  627.5 0.7 copy-start.3
  631.6 107.5 %copy-start.6 = (s32[1,3]{1,0:T(1,128)S(1)}, s32[1,3]{1,0:T(1,128)}, u32[]{:S(2)}) copy-start(s32[1,3]{1,0:T(1,128)} %param.8) | copy-start | bytes 40
  631.6 107.6 %copy-start.4 = (bf16[384,384]{0,1:T(8,128)(2,1)S(1)}, bf16[384,384]{0,1:T(8,128)(2,1)}, u32[]{:S(2)}) copy-start(bf16[384,384]{0,1:T(8,128)(2,1)} %copy-done.3) | copy-start | bytes 884740
  631.6 185.6 %all-gather.9.cloned.1.call-start = ((), (), s32[]{:S(2)}) async-start(), calls=%async_computation.5 | async-start | bytes 1671168 | tf_op jit(solution)/shard_map/all_gather | solution.py:80
  740.4 1.2 copy-start.2
Sparse Core Ops, SparseCore 0:
  10.7 207.3 all-gather.10
  220.7 242.2 all-gather.12
  466.9 157.6 all-gather.6
  631.8 103.5 reduce-scatter.1
  739.3 77.8 all-gather.8
where the time goes:
time: 828 us
  waiting for transfers between devices  660 us (80%)
  starting transfers between devices  110 us (13%)
  local copies, waits for them, and re-layouts  25.5 us (3%)
  between operations  14 us (2%)
  matrix products  10.1 us (1%)
    all_gather x1, waiting for transfers between devices, local(): lax.all_gather(qkv_bf, 'dp', axis=0, tiled=True)  208 us
    all_gather x1, waiting for transfers between devices, local(): lax.all_gather(up_bf, 'dp', axis=0, tiled=True)  185 us
    reduce_scatter x1, waiting for transfers between devices, local(): lax.psum_scatter(jnp.dot(context, dense_weight, preferred_element_type=jn...  104 us
    all_gather x1, waiting for transfers between devices, local(): normed = lax.all_gather(normed_own, 'mp', axis=0, tiled=True)  93 us
    all_gather x1, waiting for transfers between devices, local(): lax.all_gather(layer_norm(stream_own).astype(jnp.bfloat16), 'mp', axis=0,...  71.5 us
    all_to_all x1, starting transfers between devices, local(): lax.all_to_all(up_rows, 'mp', split_axis=1, concat_axis=0, tiled=True)  54.6 us
    all_to_all x1, starting transfers between devices, local(): lax.all_to_all(qkv_rows, 'mp', split_axis=1, concat_axis=0, tiled=True)  54.5 us
  transfers between devices with their start and end apart: 7, of which 5 were waited for; matrix products, arithmetic and copies ran while one was open for 4% of the time, Pallas kernels for 0%

commit v1 on v0

--- a/solution.py
+++ b/solution.py
@@ -6,6 +6,13 @@
 H = 16
 HD = 128
 PAGE = 128
+
+
+def gather_over(x, axis, along):
+    size = lax.axis_size(axis)
+    blocks = jnp.stack([x for _ in range(size)])
+    blocks = lax.all_to_all(blocks, axis, split_axis=0, concat_axis=0)
+    return jnp.concatenate(blocks, axis=along)
 
 
 def layer_norm(values):
@@ -58,7 +65,7 @@
     qkv_bf = qkv_master.astype(jnp.bfloat16)
     up_bf = up_master.astype(jnp.bfloat16)
     qkv_rows, up_rows = (
-        lax.all_gather(qkv_bf, "dp", axis=0, tiled=True),
+        gather_over(qkv_bf, "dp", 0),
         lax.all_gather(up_bf, "dp", axis=0, tiled=True),
     )
     qkv_cols, up_cols = (

time: 828 us -> 638 us (0.77)
  waiting for transfers between devices: 660 us -> 484 us
  starting transfers between devices: 110 us -> 95.6 us
    all_gather x1 -> x0, waiting for transfers between devices: 208 us -> none  [local(): lax.all_gather(qkv_bf, 'dp', axis=0, tiled=True)]
    all_to_all x0 -> x1, waiting for transfers between devices: none -> 78.3 us  [gather_over(): blocks = lax.all_to_all(blocks, axis, split_axis=0, concat_axis=0)]
    all_to_all x1, starting transfers between devices: 54.5 us -> 12.5 us  [local(): lax.all_to_all(qkv_rows, 'mp', split_axis=1, concat_axis=0, tiled=True)]
    all_gather x1, waiting for transfers between devices: 185 us -> 147 us  [local(): lax.all_gather(up_bf, 'dp', axis=0, tiled=True)]
    all_to_all x0 -> x1, starting transfers between devices: none -> 16.2 us  [gather_over(): blocks = lax.all_to_all(blocks, axis, split_axis=0, concat_axis=0)]
    all_to_all x1, starting transfers between devices: 54.6 us -> 66.6 us  [local(): lax.all_to_all(up_rows, 'mp', split_axis=1, concat_axis=0, tiled=True)]
    all_gather x1, waiting for transfers between devices: 93 us -> 83.9 us  [local(): normed = lax.all_gather(normed_own, 'mp', axis=0, tiled=True)]
  transfers between devices with their start and end apart: 7 -> 7, of which waited for: 5 -> 5; matrix products, arithmetic and copies ran while one was open for 4% -> 5% of each run, Pallas kernels for 0% -> 0%
where the time goes in v1:
time: 638 us; the launch traced here: 637 us
  waiting for transfers between devices  484 us (76%)
  starting transfers between devices  95.6 us (15%)
  local copies, waits for them, and re-layouts  27.6 us (4%)
  between operations  14 us (2%)
  matrix products  9.42 us (1%)
  other arithmetic  6.65 us (1%)
    all_gather x1, waiting for transfers between devices, local(): lax.all_gather(up_bf, 'dp', axis=0, tiled=True)  147 us
    reduce_scatter x1, waiting for transfers between devices, local(): lax.psum_scatter(jnp.dot(context, dense_weight, preferred_element_type=jn...  103 us
    all_gather x1, waiting for transfers between devices, local(): normed = lax.all_gather(normed_own, 'mp', axis=0, tiled=True)  83.9 us
    all_to_all x1, waiting for transfers between devices, gather_over(): blocks = lax.all_to_all(blocks, axis, split_axis=0, concat_axis=0)  78.3 us
    all_gather x1, waiting for transfers between devices, local(): lax.all_gather(layer_norm(stream_own).astype(jnp.bfloat16), 'mp', axis=0,...  71.6 us
    all_to_all x1, starting transfers between devices, local(): lax.all_to_all(up_rows, 'mp', split_axis=1, concat_axis=0, tiled=True)  66.6 us
    all_to_all x1, starting transfers between devices, gather_over(): blocks = lax.all_to_all(blocks, axis, split_axis=0, concat_axis=0)  16.2 us
  transfers between devices with their start and end apart: 7, of which 5 were waited for; matrix products, arithmetic and copies ran while one was open for 5% of the time, Pallas kernels for 0%

profile of v1, /device:TPU:1, one launch (start us, length us, event | category | flops | bytes accessed | tf_op | source)
XLA Modules:
  0.0 637.2 jit_solution(4843343853089383723)
XLA Ops:
  7.2 0.0 copy-start
  7.2 1.0 convert_element_type.55
  8.2 1.9 stack.4
  10.0 16.2 %all-to-all-start = ((bf16[32,4,6144]{2,1,0:T(4,128)(2,1)}), bf16[32,4,6144]{2,1,0:T(4,128)(2,1)S(1)}, u32[]{:S(2)}, u32[]{:S(2)}) async-start(bf16[32,4,6144]{2,1,0:T(4,128)(2,1)} %stack.4), calls=%async_computation | async-start | bytes 3145728 | tf_op jit(solution)/shard_map/all_to_all | solution.py:14
  26.2 0.0 all-gather.9.cloned.1.call-start
  26.3 0.7 convert_bitcast_fusion
  27.0 0.0 all-gather.9.cloned.1.call-update
  27.0 78.3 %all-to-all-done = bf16[32,4,6144]{2,1,0:T(4,128)(2,1)S(1)} async-done(((bf16[32,4,6144]{2,1,0:T(4,128)(2,1)}), bf16[32,4,6144]{2,1,0:T(4,128)(2,1)S(1)}, u32[]{:S(2)}, u32[]{:S(2)}) %all-to-all-start) | async-done | bytes 1572896 | tf_op jit(solution)/shard_map/all_to_all | solution.py:14
  105.3 1.9 all_to_all.28
  107.2 2.9 copy.29
  110.1 12.5 %all-to-all-start.1 = ((bf16[128,16,384]{2,0,1:T(8,128)(2,1)}), bf16[128,16,384]{2,0,1:T(8,128)(2,1)}, u32[]{:S(2)}, u32[]{:S(2)}) async-start(bf16[128,16,384]{2,0,1:T(8,128)(2,1)} %copy.29), calls=%async_computation.1 | async-start | bytes 3145728 | tf_op jit(solution)/shard_map/all_to_all | solution.py:72
  122.6 0.0 all-gather.5.cloned.1.call-start
  122.6 0.1 convert_reduce_fusion
  122.8 0.2 fusion.19
  123.0 0.7 fusion.20
  123.7 0.0 all-gather.5.cloned.1.call-update
  123.8 146.6 %all-gather.9.cloned.1.call-done = bf16[32,4,8192]{2,1,0:T(4,128)(2,1)} async-done(((bf16[1,4,8192]{2,1,0:T(4,128)(2,1)}), bf16[32,4,8192]{2,1,0:T(4,128)(2,1)}) %all-gather.9.cloned.1.call-update) | async-done | bytes 2097168 | tf_op jit(solution)/shard_map/all_gather | solution.py:69
  270.3 3.3 all_to_all.31
  273.6 2.5 copy.34
  276.1 66.6 %all-to-all-start.2 = ((bf16[128,16,512]{2,0,1:T(8,128)(2,1)}), bf16[128,16,512]{2,0,1:T(8,128)(2,1)S(1)}, u32[]{:S(2)}, u32[]{:S(2)}) async-start(bf16[128,16,512]{2,0,1:T(8,128)(2,1)} %copy.34), calls=%async_computation.3 | async-start | bytes 4194304 | tf_op jit(solution)/shard_map/all_to_all | solution.py:73
  342.7 0.0 reduce-scatter.2.cloned.1.call-start
  342.8 2.3 copy.30
  345.1 2.0 copy.31
  347.1 3.7 reshape.138
  350.9 83.9 %all-gather.5.cloned.1.call-done = bf16[384,2048]{1,0:T(8,128)(2,1)} async-done(((bf16[24,2048]{1,0:T(8,128)(2,1)}), bf16[384,2048]{1,0:T(8,128)(2,1)}) %all-gather.5.cloned.1.call-update) | async-done | bytes 1572880 | tf_op jit(solution)/shard_map/all_gather | solution.py:78
  434.8 2.9 convolution_convert_fusion.1
  437.7 0.0 copy-start.4
  437.7 0.7 copy-done.4
  438.4 0.4 fusion.31
  438.8 0.1 fusion.12
  438.9 2.8 convolution_convert_fusion
  441.8 0.0 reduce-scatter.2.cloned.1.call-update
  441.8 0.2 all-gather.7.cloned.1.call-start
  442.0 103.5 %reduce-scatter.2.cloned.1.call-done = bf16[24,2048]{1,0:T(8,128)(2,1)} async-done(((bf16[384,2048]{1,0:T(8,128)(2,1)}), bf16[24,2048]{1,0:T(8,128)(2,1)}) %reduce-scatter.2.cloned.1.call-update) | async-done | bytes 98320 | tf_op jit(solution)/shard_map/reduce_scatter | solution.py:80
  545.5 1.0 fusion.21
  546.5 1.1 multiply_reduce_fusion
  547.6 1.6 multiply_convert_fusion
  549.3 0.0 all-gather.7.cloned.1.call-update
  549.3 1.2 copy.35
  550.5 2.0 copy.36
  552.5 0.0 copy-start.5
  552.5 2.1 reshape.145
  554.6 0.1 copy.39
  554.7 0.1 copy.40
  554.9 0.8 scatter_fusion
  555.8 0.0 copy-start.3
  555.8 71.6 %all-gather.7.cloned.1.call-done = bf16[384,2048]{1,0:T(8,128)(2,1)} async-done(((bf16[24,2048]{1,0:T(8,128)(2,1)}), bf16[384,2048]{1,0:T(8,128)(2,1)}) %all-gather.7.cloned.1.call-update) | async-done | bytes 1572880 | tf_op jit(solution)/shard_map/all_gather | solution.py:87
  627.4 3.3 fusion.10
  (25 shorter events, 0.2 us)
Async XLA Ops:
  7.2 431.7 %copy-start = (bf16[128,2048]{1,0:T(8,128)(2,1)S(1)}, bf16[128,2048]{1,0:T(8,128)(2,1)}, u32[]{:S(2)}) copy-start(bf16[128,2048]{1,0:T(8,128)(2,1)} %param.11) | copy-start | bytes 1572868
  10.0 16.3 %copy-start.6 = (f32[4,8192]{1,0:T(4,128)S(1)}, f32[4,8192]{1,0:T(4,128)}, u32[]{:S(2)}) copy-start(f32[4,8192]{1,0:T(4,128)} %param.10) | copy-start | bytes 393220
  10.0 95.3 %all-to-all-start = ((bf16[32,4,6144]{2,1,0:T(4,128)(2,1)}), bf16[32,4,6144]{2,1,0:T(4,128)(2,1)S(1)}, u32[]{:S(2)}, u32[]{:S(2)}) async-start(bf16[32,4,6144]{2,1,0:T(4,128)(2,1)} %stack.4), calls=%async_computation | async-start | bytes 3145728 | tf_op jit(solution)/shard_map/all_to_all | solution.py:14
  26.2 244.1 %all-gather.9.cloned.1.call-start = ((), (), s32[]{:S(2)}) async-start(), calls=%async_computation.7 | async-start | bytes 2162688 | tf_op jit(solution)/shard_map/all_gather | solution.py:69
  110.1 12.5 %copy-start.1 = (bf16[24,2048]{1,0:T(8,128)(2,1)S(1)}, bf16[24,2048]{1,0:T(8,128)(2,1)}, u32[]{:S(2)}) copy-start(bf16[24,2048]{1,0:T(8,128)(2,1)} %param.6) | copy-start | bytes 294916
  110.1 166.0 %all-to-all-start.1 = ((bf16[128,16,384]{2,0,1:T(8,128)(2,1)}), bf16[128,16,384]{2,0,1:T(8,128)(2,1)}, u32[]{:S(2)}, u32[]{:S(2)}) async-start(bf16[128,16,384]{2,0,1:T(8,128)(2,1)} %copy.29), calls=%async_computation.1 | async-start | bytes 3145728 | tf_op jit(solution)/shard_map/all_to_all | solution.py:72
  122.6 312.2 %all-gather.5.cloned.1.call-start = ((), (), s32[]{:S(2)}) async-start(), calls=%async_computation.4 | async-start | bytes 1671168 | tf_op jit(solution)/shard_map/all_gather | solution.py:78
  276.1 66.7 %copy-start.7 = (s32[1,384]{1,0:T(1,128)S(1)}, s32[1,384]{1,0:T(1,128)}, u32[]{:S(2)}) copy-start(s32[1,384]{1,0:T(1,128)} %param.7) | copy-start | bytes 4612
  276.1 273.2 %all-to-all-start.2 = ((bf16[128,16,512]{2,0,1:T(8,128)(2,1)}), bf16[128,16,512]{2,0,1:T(8,128)(2,1)S(1)}, u32[]{:S(2)}, u32[]{:S(2)}) async-start(bf16[128,16,512]{2,0,1:T(8,128)(2,1)} %copy.34), calls=%async_computation.3 | async-start | bytes 4194304 | tf_op jit(solution)/shard_map/all_to_all | solution.py:73
  342.7 202.8 %reduce-scatter.2.cloned.1.call-start = ((), (), s32[]{:S(2)}) async-start(), calls=%async_computation.5 | async-start | bytes 1671168 | tf_op jit(solution)/shard_map/reduce_scatter | solution.py:80
  437.7 0.7 copy-start.4
  441.8 107.5 %copy-start.8 = (s32[1,3]{1,0:T(1,128)S(1)}, s32[1,3]{1,0:T(1,128)}, u32[]{:S(2)}) copy-start(s32[1,3]{1,0:T(1,128)} %param.8) | copy-start | bytes 40
  441.8 185.6 %all-gather.7.cloned.1.call-start = ((), (), s32[]{:S(2)}) async-start(), calls=%async_computation.6 | async-start | bytes 1671168 | tf_op jit(solution)/shard_map/all_gather | solution.py:87
  552.5 2.1 copy-start.5
  554.6 72.8 %copy-start.2 = (bf16[2048,512]{1,0:T(8,128)(2,1)S(1)}, bf16[2048,512]{1,0:T(8,128)(2,1)}, u32[]{:S(2)}) copy-start(bf16[2048,512]{1,0:T(8,128)(2,1)} %reshape.145) | copy-start | bytes 6291460
  555.8 74.9 %copy-start.3 = (bf16[3,2,128,128]{3,2,1,0:T(8,128)(2,1)}, bf16[3,2,128,128]{3,2,1,0:T(8,128)(2,1)S(1)}, u32[]{:S(2)}) copy-start(bf16[3,2,128,128]{3,2,1,0:T(8,128)(2,1)S(1)} %scatter_fusion) | copy-start | bytes 589828
Sparse Core Ops, SparseCore 0:
  29.7 240.5 all-gather.8
  274.2 160.4 all-gather.4
  441.9 103.5 reduce-scatter.1
  549.4 77.8 all-gather.6
